TPU v7x, 256 devices: a whole 4x4x8 slice. The times are simulated.
256 devices in a mesh: pb: 16 (over z, core), kv: 16 (over y, x).
Axes of the slice: x: 4, y: 4, z: 8, core: 2. Of those that a mesh axis runs over, the one named last changes fastest.
Arguments:
- queries: bfloat16 [393216, 1024], P(('pb', 'kv')), may hold values from -8 to 8
- keys: bfloat16 [524288, 128], P(('kv', 'pb')), may hold values from -6 to 6
- values: bfloat16 [524288, 128], P(('kv', 'pb')), may hold values from -6 to 6
- selected: int32 [6144, 14], P(('pb', 'kv')), may hold values from 1 to 8190, as said below
Outputs:
- attended: bfloat16 [393216, 1024], P(('pb', 'kv'))
Inputs may be any that keep to these rules, and one draw needn't show every extreme that they name: `selected`: each row names 14 different blocks, never block 0 or block 8191. Key device k holds blocks k * 32 to (k + 1) * 32 - 1, devices counted with kv slowest; query device d holds query blocks d * 24 to (d + 1) * 24 - 1, devices counted with pb slowest. The query blocks of one device name together at most 2 distinct blocks of one key device, and in every draw some key device has exactly 2 named by every query device.
All inputs are finite; a program needn't handle non-finite values.
Results may differ from a plain program's by a relative error of at most 0.0046.
Values may be sent and summed in bfloat16 or wider, within the bound.
A program may use at most 128 MiB of HBM per device.

v0:
```python
import math
import jax
import jax.numpy as jnp
from jax import lax
from jax.sharding import PartitionSpec as P

H = 8
DH = 128
BLOCK = 64
TOPN = 16
QB = 64
CAP = 2


def holdings(wanted, owner, blocks_here):
    local_ids = owner * blocks_here + jnp.arange(blocks_here, dtype=jnp.int32)
    hits = (wanted[:, None] == local_ids[None, :]).astype(jnp.int32)
    present = jnp.max(hits, axis=0)
    return (present, jnp.cumsum(present) - present)


def slot_lists(present, slot_rank, slots):
    local_ids = jnp.arange(present.shape[-1], dtype=jnp.int32)
    slot_ids = jnp.arange(slots, dtype=jnp.int32)
    matches = (present[..., :, None] == 1) & (slot_rank[..., :, None] == slot_ids)
    return jnp.sum(jnp.where(matches, local_ids[:, None], 0), axis=-2)


def per_device(queries, keys, values, selected):
    pb_count = lax.axis_size("pb")
    kv_count = lax.axis_size("kv")
    devices = pb_count * kv_count
    blocks_here = keys.shape[0] // BLOCK
    query_blocks = queries.shape[0] // QB
    column_blocks = pb_count * blocks_here
    tiles_local = jnp.concatenate(
        [keys.reshape(blocks_here, BLOCK, DH), values.reshape(blocks_here, BLOCK, DH)], axis=2
    )
    column = lax.all_gather(tiles_local, "pb", axis=0, tiled=True)
    slots = CAP
    wanted = selected.reshape(-1)
    owners = jnp.arange(devices, dtype=jnp.int32)
    present, slot_rank = jax.vmap(lambda owner: holdings(wanted, owner, blocks_here))(owners)
    owner_lists = slot_lists(present, slot_rank, slots)
    by_column = (
        owner_lists.reshape(kv_count, pb_count, slots)
        + jnp.arange(pb_count, dtype=jnp.int32)[None, :, None] * blocks_here
    )
    by_column = by_column.reshape(kv_count, pb_count * slots)
    asked_for = lax.all_to_all(by_column, "kv", split_axis=0, concat_axis=0, tiled=True)
    outgoing = jnp.take(column, asked_for.reshape(-1), axis=0).reshape(
        kv_count, pb_count * slots, BLOCK, 2 * DH
    )
    fetched = lax.all_to_all(outgoing, "kv", split_axis=0, concat_axis=0, tiled=True)
    tile_table = fetched.reshape(devices * slots, BLOCK, 2 * DH)
    owner_of = selected // blocks_here
    positions = owner_of * slots + jnp.take(slot_rank.reshape(-1), selected)
    me_kv = lax.axis_index("kv")
    ends = jnp.concatenate([column[:1], column[column_blocks - 1 :]], axis=0)
    ends = jnp.where(
        jnp.stack([me_kv == 0, me_kv == kv_count - 1])[:, None, None], ends, jnp.zeros_like(ends)
    )
    ends = lax.psum(ends, "kv")
    tile_table = jnp.concatenate([tile_table, ends], axis=0)
    extra_base = devices * slots
    leading_positions = jnp.broadcast_to(
        jnp.array([extra_base, extra_base + 1], jnp.int32), (query_blocks, 2)
    )
    positions = jnp.concatenate([leading_positions, positions], axis=1)
    group_size = math.gcd(query_blocks, 8)
    q_groups = queries.reshape(query_blocks // group_size, group_size, QB * H, DH)
    p_groups = positions.reshape(query_blocks // group_size, group_size, TOPN)

    def attend(operands):
        q_block, positions_in = operands
        gathered = jnp.take(tile_table, positions_in.reshape(-1), axis=0).reshape(
            group_size, TOPN * BLOCK, 2 * DH
        )
        scores = jnp.einsum(
            "gqd,gkd->gqk", q_block, gathered[..., :DH], preferred_element_type=jnp.float32
        ) * DH ** (-0.5)
        weights = jnp.exp(scores - jnp.max(scores, axis=-1, keepdims=True))
        totals = jnp.sum(weights, axis=-1, keepdims=True)
        weighted = jnp.einsum(
            "gqk,gkd->gqd",
            weights.astype(jnp.bfloat16),
            gathered[..., DH:],
            preferred_element_type=jnp.float32,
        )
        return (weighted / totals).astype(jnp.bfloat16)

    result = lax.map(attend, (q_groups, p_groups))
    return result.reshape(query_blocks * QB, H * DH)


def solution(mesh):
    placed = (
        P(("pb", "kv"), None),
        P(("kv", "pb"), None),
        P(("kv", "pb"), None),
        P(("pb", "kv"), None),
    )
    return jax.shard_map(
        per_device, mesh=mesh, in_specs=placed, out_specs=P(("pb", "kv"), None), check_vma=False
    )
```

profile of v0, /device:TPU:2, one launch (start us, length us, event | category | flops | bytes accessed | tf_op | source)
XLA Modules:
  0.0 519.4 jit_solution(11960891043452149832)
XLA Ops:
  6.5 0.0 all-gather.2.cloned.1.call-start
  6.5 2.3 pad_maximum_fusion.1
  8.9 0.0 all-gather.2.cloned.1.call-update
  8.9 0.1 add.104
  9.0 0.1 add.105
  9.0 0.8 copy.30
  9.8 0.1 eq.45
  9.9 1.7 convert_reduce_fusion
  11.7 0.1 reduce_window_sum.11
  11.8 0.1 copy.38
  11.9 0.1 reshape.205
  12.1 13.5 %all_to_all.11 = s32[16,1,32]{2,1,0:T(1,128)S(1)} all-to-all(s32[16,1,32]{2,1,0:T(1,128)S(1)} %bitcast.44), channel_id=1, replica_groups=mesh['pb'=16,'kv'=16] {'kv'}, dimensions={0} | all-to-all | bytes 4096 | tf_op jit(solution)/shard_map/all_to_all | solution.py:50
  25.5 0.5 broadcast.157
  26.0 0.6 reduce.3
  26.6 0.1 reshape.209
  26.7 80.8 %all-gather.2.cloned.1.call-done = bf16[512,64,256]{2,1,0:T(8,128)(2,1)} async-done(((bf16[32,64,256]{2,1,0:T(8,128)(2,1)}), bf16[512,64,256]{2,1,0:T(8,128)(2,1)}) %all-gather.2.cloned.1.call-update) | async-done | bytes 16777232 | tf_op jit(solution)/shard_map/all_gather | solution.py:39
  107.6 19.5 %gather_fusion.2 = bf16[512,64,256]{2,1,0:T(8,128)(2,1)} fusion(bf16[512,64,256]{2,1,0:T(8,128)(2,1)} %all-gather.2.cloned.1.call-done, s32[1024]{0:T(1024)S(1)} %pad_clamp_fusion.1), kind=kCustom, calls=%fused_computation.2 | custom fusion | bytes 33556480 | tf_op jit(solution)/shard_map/jit(_take)/gather | solution.py:51
  127.0 14.1 %broadcast_select_fusion = bf16[16,32,64,256]{3,2,1,0:T(8,128)(2,1)} fusion(bf16[16,32,64,256]{3,2,1,0:T(8,128)(2,1)} %bitcast.40, pred[16,32]{1,0:T(8,128)(4,1)S(1)} %compare_and_fusion.1), kind=kLoop, calls=%fused_computation.27 | loop fusion | flops 8388608 | bytes 33554944 | tf_op jit(solution)/shard_map/jit(_take)/select_n | solution.py:51
  141.2 0.0 copy-start
  141.2 7.4 %all-to-all-start.1 = ((bf16[16,32,64,256]{3,2,1,0:T(8,128)(2,1)}), bf16[16,32,64,256]{3,2,1,0:T(8,128)(2,1)}, u32[]{:S(2)}, u32[]{:S(2)}) async-start(bf16[16,32,64,256]{3,2,1,0:T(8,128)(2,1)} %broadcast_select_fusion), calls=%async_computation.1 | async-start | bytes 33554432 | tf_op jit(solution)/shard_map/all_to_all | solution.py:54
  148.6 0.0 all-reduce.2.cloned.1.call-start
  148.6 0.1 copy.37
  148.7 0.0 copy-done
  148.8 0.1 reshape.222
  148.9 0.1 sub.27
  149.0 2.5 gather_fusion.1
  151.5 0.1 reshape.221
  151.6 0.1 pad_add_fusion
  151.7 0.8 fusion.23
  152.5 0.7 maximum_select_fusion
  153.2 0.0 all-reduce.2.cloned.1.call-update
  153.2 0.1 add_bitcast_fusion
  153.3 4.1 reshape.203
  157.4 264.4 %all-reduce.2.cloned.1.call-done = bf16[2,64,256]{2,1,0:T(8,128)(2,1)} async-done(((bf16[2,64,256]{2,1,0:T(8,128)(2,1)}), bf16[2,64,256]{2,1,0:T(8,128)(2,1)}) %all-reduce.2.cloned.1.call-update) | async-done | bytes 65552 | tf_op jit(solution)/shard_map/psum | solution.py:63
  421.9 0.0 all-to-all-done.1
  421.9 14.1 %pad_maximum_fusion = bf16[514,64,256]{2,1,0:T(8,128)(2,1)} fusion(bf16[2,64,256]{2,1,0:T(8,128)(2,1)} %all-reduce.2.cloned.1.call-done, bf16[512,64,256]{2,1,0:T(8,128)(2,1)} %bitcast.12), kind=kLoop, calls=%fused_computation.26 | loop fusion | flops 8421376 | bytes 33685504 | tf_op jit(solution)/shard_map/concatenate | solution.py:64
  436.0 70.9 %while.10 = (s32[]{:T(128)}, bf16[3,8,512,128]{3,2,1,0:T(8,128)(2,1)}, bf16[3,8,512,128]{3,2,1,0:T(8,128)(2,1)S(1)}, s32[3,8,16]{2,1,0:T(8,128)S(1)}, bf16[514,64,256]{2,1,0:T(8,128)(2,1)}, /*index=5*/s32[]{:T(128)}) while((s32[]{:T(128)}, bf16[3,8,512,128]{3,2,1,0:T(8,128)(2,1)}, bf16[3,8,512,128]{3,2,1,0:T(8,128)(2,1)S(1)}, ...), condition=%wide.region_7.8_spmd, body=%wide.region_4.7_spmd.sunk | while | flops 2184177664 | bytes 73523544 | solution.py:92
  436.0 0.1 reshape.253
  436.1 0.1 broadcast_in_dim.101
  436.2 0.1 broadcast_in_dim.102
  436.3 8.5 %gather_fusion = bf16[128,64,256]{2,1,0:T(8,128)(2,1)} fusion(bf16[514,64,256]{2,1,0:T(8,128)(2,1)} %get-tuple-element.104, s32[1024]{0:T(1024)S(1)} %pad_clamp_fusion.4), kind=kCustom, calls=%fused_computation.clone.1 | custom fusion | bytes 8389120 | tf_op jit(solution)/shard_map/while/body/eval_jaxpr/jit(_take)/gather | solution.py:76
  444.8 4.6 bitcast_select_fusion.2
  449.4 2.4 multiply_reduce_fusion.2
  451.8 3.5 fusion.31
  455.3 4.2 bitcast_dynamic-update-slice_fusion.2
  459.6 0.1 reshape.253
  459.7 0.1 broadcast_in_dim.101
  459.8 0.1 broadcast_in_dim.102
  459.9 8.5 %gather_fusion = bf16[128,64,256]{2,1,0:T(8,128)(2,1)} fusion(bf16[514,64,256]{2,1,0:T(8,128)(2,1)} %get-tuple-element.104, s32[1024]{0:T(1024)S(1)} %pad_clamp_fusion.4), kind=kCustom, calls=%fused_computation.clone.1 | custom fusion | bytes 8389120 | tf_op jit(solution)/shard_map/while/body/eval_jaxpr/jit(_take)/gather | solution.py:76
  468.4 4.6 bitcast_select_fusion.2
  473.0 2.4 multiply_reduce_fusion.2
  475.4 3.5 fusion.31
  479.0 4.2 bitcast_dynamic-update-slice_fusion.2
  483.2 0.1 reshape.253
  483.3 0.1 broadcast_in_dim.101
  483.4 0.1 broadcast_in_dim.102
  483.5 8.5 %gather_fusion = bf16[128,64,256]{2,1,0:T(8,128)(2,1)} fusion(bf16[514,64,256]{2,1,0:T(8,128)(2,1)} %get-tuple-element.104, s32[1024]{0:T(1024)S(1)} %pad_clamp_fusion.4), kind=kCustom, calls=%fused_computation.clone.1 | custom fusion | bytes 8389120 | tf_op jit(solution)/shard_map/while/body/eval_jaxpr/jit(_take)/gather | solution.py:76
  492.0 4.6 bitcast_select_fusion.2
  496.6 2.4 multiply_reduce_fusion.2
  499.0 3.5 fusion.31
  502.6 4.2 bitcast_dynamic-update-slice_fusion.2
  506.8 5.8 %reshape.211 = bf16[1536,1024]{1,0:T(8,128)(2,1)} reshape(bf16[3,8,512,128]{3,2,1,0:T(8,128)(2,1)} %get-tuple-element.32) | data formatting | bytes 6291456 | tf_op jit(solution)/shard_map/reshape | solution.py:93
  (24 shorter events, 0.2 us)
Async XLA Ops:
  6.5 101.0 %all-gather.2.cloned.1.call-start = ((), (), s32[]{:S(2)}) async-start(), calls=%async_computation.2 | async-start | bytes 17825792 | tf_op jit(solution)/shard_map/all_gather | solution.py:39
  141.2 7.5 %copy-start = (s32[2]{0:T(128)S(1)}, s32[2]{0:T(128)}, u32[]{:S(2)}) copy-start(s32[2]{0:T(128)} %constant.100.clone) | copy-start | bytes 28
  141.2 280.7 %all-to-all-start.1 = ((bf16[16,32,64,256]{3,2,1,0:T(8,128)(2,1)}), bf16[16,32,64,256]{3,2,1,0:T(8,128)(2,1)}, u32[]{:S(2)}, u32[]{:S(2)}) async-start(bf16[16,32,64,256]{3,2,1,0:T(8,128)(2,1)} %broadcast_select_fusion), calls=%async_computation.1 | async-start | bytes 33554432 | tf_op jit(solution)/shard_map/all_to_all | solution.py:54
  148.6 273.3 %all-reduce.2.cloned.1.call-start = ((), (), s32[]{:S(2)}) async-start(), calls=%async_computation.3 | async-start | bytes 131072 | tf_op jit(solution)/shard_map/psum | solution.py:63
Sparse Core Ops, SparseCore 0:
  9.2 98.3 all-gather.1
  153.3 268.4 all-reduce.1
where the time goes:
time: 521 us; the launch traced here: 519 us
  waiting for transfers between devices  345 us (66%)
  local copies, waits for them, and re-layouts  61.3 us (12%)
  other arithmetic  58.3 us (11%)
  matrix products  20 us (4%)
  between operations  13.6 us (3%)
  blocking collectives  13.5 us (3%)
  starting transfers between devices  7.43 us (1%)
    psum x1, waiting for transfers between devices, per_device(): ends = lax.psum(ends, 'kv')  264 us
    all_gather x1, waiting for transfers between devices, per_device(): column = lax.all_gather(tiles_local, 'pb', axis=0, tiled=True)  80.8 us
    gather x3, local copies, waits for them, and re-layouts, attend(): jnp.take(tile_table, positions_in.reshape(-1), axis=0)  25.6 us
    gather x1, local copies, waits for them, and re-layouts, per_device(): jnp.take(column, asked_for.reshape(-1), axis=0)  19.5 us
    select_n x2, other arithmetic, per_device(): jnp.take(column, asked_for.reshape(-1), axis=0)  14.1 us
    concatenate x1, other arithmetic, per_device(): tile_table = jnp.concatenate([tile_table, ends], axis=0)  14.1 us
    select_n x6, other arithmetic, attend(): jnp.take(tile_table, positions_in.reshape(-1), axis=0)  13.7 us
    all_to_all x1, blocking collectives, per_device(): lax.all_to_all(by_column, 'kv', split_axis=0, concat_axis=0, tiled=True)  13.5 us
  transfers between devices with their start and end apart: 3, of which 2 were waited for; matrix products, arithmetic and copies ran while one was open for 3% of the time, Pallas kernels for 0%

commit v1 on v0

--- a/solution.py
+++ b/solution.py
@@ -36,7 +36,9 @@
     tiles_local = jnp.concatenate(
         [keys.reshape(blocks_here, BLOCK, DH), values.reshape(blocks_here, BLOCK, DH)], axis=2
     )
-    column = lax.all_gather(tiles_local, "pb", axis=0, tiled=True)
+    column = jnp.concatenate(
+        lax.all_to_all(jnp.stack([tiles_local] * lax.axis_size("pb")), "pb", 0, 0), axis=0
+    )
     slots = CAP
     wanted = selected.reshape(-1)
     owners = jnp.arange(devices, dtype=jnp.int32)

time: 521 us -> 816 us (1.57)
  waiting for transfers between devices: 345 us -> 633 us
  starting transfers between devices: 7.43 us -> 22.6 us
  blocking collectives: 13.5 us -> 0 us
    all_to_all x0 -> x2, waiting for transfers between devices: none -> 367 us  [the longest x1 363 us: per_device(): lax.all_to_all(jnp.stack([tiles_local] * lax.axis_size('pb')), 'pb', 0, 0)]
    all_gather x1 -> x0, waiting for transfers between devices: 80.8 us -> none  [per_device(): column = lax.all_gather(tiles_local, 'pb', axis=0, tiled=True)]
    all_to_all x0 -> x2, starting transfers between devices: none -> 16.1 us  [the longest x1 8.62 us: per_device(): lax.all_to_all(jnp.stack([tiles_local] * lax.axis_size('pb')), 'pb', 0, 0)]
    all_to_all x1 -> x0, blocking collectives: 13.5 us -> none  [per_device(): lax.all_to_all(by_column, 'kv', split_axis=0, concat_axis=0, tiled=True)]
  transfers between devices with their start and end apart: 3 -> 4, of which waited for: 2 -> 3; matrix products, arithmetic and copies ran while one was open for 3% -> 1% of each run, Pallas kernels for 0% -> 0%
where the time goes in v1:
time: 816 us; the launch traced here: 815 us
  waiting for transfers between devices  633 us (78%)
  local copies, waits for them, and re-layouts  67.3 us (8%)
  other arithmetic  58 us (7%)
  starting transfers between devices  22.6 us (3%)
  matrix products  20 us (2%)
  between operations  13.6 us (2%)
    all_to_all x1, waiting for transfers between devices, per_device(): lax.all_to_all(jnp.stack([tiles_local] * lax.axis_size('pb')), 'pb', 0, 0)  363 us
    psum x1, waiting for transfers between devices, per_device(): ends = lax.psum(ends, 'kv')  266 us
    gather x3, local copies, waits for them, and re-layouts, attend(): jnp.take(tile_table, positions_in.reshape(-1), axis=0)  25.6 us
    gather x1, local copies, waits for them, and re-layouts, per_device(): jnp.take(column, asked_for.reshape(-1), axis=0)  19.5 us
  transfers between devices with their start and end apart: 4, of which 3 were waited for; matrix products, arithmetic and copies ran while one was open for 1% of the time, Pallas kernels for 0%

profile of v1, /device:TPU:2, one launch (start us, length us, event | category | flops | bytes accessed | tf_op | source)
XLA Modules:
  0.0 814.7 jit_solution(3307979428406778152)
XLA Ops:
  6.5 0.1 add.104
  6.6 0.1 add.105
  6.7 0.8 copy.30
  7.5 0.1 eq.45
  7.6 1.7 convert_reduce_fusion
  9.3 0.1 reduce_window_sum.11
  9.4 0.1 copy.38
  9.6 0.1 reshape.210
  9.7 0.6 broadcast_add_fusion
  10.3 7.5 all-to-all-start
  17.8 1.3 pad_maximum_fusion.1
  19.1 4.8 all-to-all-done
  23.9 5.9 stack.8
  29.8 8.6 %all-to-all-start.1 = ((bf16[16,32,64,256]{3,2,1,0:T(8,128)(2,1)}), bf16[16,32,64,256]{3,2,1,0:T(8,128)(2,1)}, u32[]{:S(2)}, u32[]{:S(2)}) async-start(bf16[16,32,64,256]{3,2,1,0:T(8,128)(2,1)} %stack.8), calls=%async_computation.1 | async-start | bytes 33554432 | tf_op jit(solution)/shard_map/all_to_all | solution.py:40
  38.5 0.5 broadcast.159
  39.0 0.7 reduce.3
  39.7 0.1 reshape.215
  39.8 362.7 %all-to-all-done.1 = bf16[16,32,64,256]{3,2,1,0:T(8,128)(2,1)} async-done(((bf16[16,32,64,256]{3,2,1,0:T(8,128)(2,1)}), bf16[16,32,64,256]{3,2,1,0:T(8,128)(2,1)}, u32[]{:S(2)}, u32[]{:S(2)}) %all-to-all-start.1) | async-done | bytes 16777248 | tf_op jit(solution)/shard_map/all_to_all | solution.py:40
  402.4 19.5 %gather_fusion.2 = bf16[512,64,256]{2,1,0:T(8,128)(2,1)} fusion(bf16[512,64,256]{2,1,0:T(8,128)(2,1)} %bitcast.10, s32[1024]{0:T(1024)S(1)} %pad_clamp_fusion.1), kind=kCustom, calls=%fused_computation.2 | custom fusion | bytes 33556480 | tf_op jit(solution)/shard_map/jit(_take)/gather | solution.py:53
  421.9 14.1 %broadcast_select_fusion = bf16[16,32,64,256]{3,2,1,0:T(8,128)(2,1)} fusion(bf16[16,32,64,256]{3,2,1,0:T(8,128)(2,1)} %bitcast.41, pred[16,32]{1,0:T(8,128)(4,1)S(1)} %compare_and_fusion.1), kind=kLoop, calls=%fused_computation.27 | loop fusion | flops 8388608 | bytes 33554944 | tf_op jit(solution)/shard_map/jit(_take)/select_n | solution.py:53
  436.0 0.0 copy-start
  436.0 6.5 all-to-all-start.2
  442.5 0.0 all-reduce.2.cloned.1.call-start
  442.6 0.1 copy.37
  442.7 0.0 copy-done
  442.7 0.1 reshape.228
  442.8 0.1 sub.27
  442.9 2.5 gather_fusion.1
  445.5 0.1 reshape.227
  445.5 0.1 pad_add_fusion
  445.6 0.8 fusion.23
  446.4 0.7 maximum_select_fusion
  447.1 0.0 all-reduce.2.cloned.1.call-update
  447.2 0.1 add_bitcast_fusion
  447.2 4.1 reshape.208
  451.4 265.7 %all-reduce.2.cloned.1.call-done = bf16[2,64,256]{2,1,0:T(8,128)(2,1)} async-done(((bf16[2,64,256]{2,1,0:T(8,128)(2,1)}), bf16[2,64,256]{2,1,0:T(8,128)(2,1)}) %all-reduce.2.cloned.1.call-update) | async-done | bytes 65552 | tf_op jit(solution)/shard_map/psum | solution.py:65
  717.1 0.0 all-to-all-done.2
  717.1 14.1 %pad_maximum_fusion = bf16[514,64,256]{2,1,0:T(8,128)(2,1)} fusion(bf16[2,64,256]{2,1,0:T(8,128)(2,1)} %all-reduce.2.cloned.1.call-done, bf16[512,64,256]{2,1,0:T(8,128)(2,1)} %bitcast.13), kind=kLoop, calls=%fused_computation.26 | loop fusion | flops 8421376 | bytes 33685504 | tf_op jit(solution)/shard_map/concatenate | solution.py:66
  731.2 70.9 %while.10 = (s32[]{:T(128)}, bf16[3,8,512,128]{3,2,1,0:T(8,128)(2,1)}, bf16[3,8,512,128]{3,2,1,0:T(8,128)(2,1)S(1)}, s32[3,8,16]{2,1,0:T(8,128)S(1)}, bf16[514,64,256]{2,1,0:T(8,128)(2,1)}, /*index=5*/s32[]{:T(128)}) while((s32[]{:T(128)}, bf16[3,8,512,128]{3,2,1,0:T(8,128)(2,1)}, bf16[3,8,512,128]{3,2,1,0:T(8,128)(2,1)S(1)}, ...), condition=%wide.region_7.8_spmd, body=%wide.region_4.7_spmd.sunk | while | flops 2184177664 | bytes 73523544 | solution.py:94
  731.2 0.1 reshape.259
  731.3 0.1 broadcast_in_dim.101
  731.4 0.1 broadcast_in_dim.102
  731.5 8.5 %gather_fusion = bf16[128,64,256]{2,1,0:T(8,128)(2,1)} fusion(bf16[514,64,256]{2,1,0:T(8,128)(2,1)} %get-tuple-element.104, s32[1024]{0:T(1024)S(1)} %pad_clamp_fusion.4), kind=kCustom, calls=%fused_computation.clone.1 | custom fusion | bytes 8389120 | tf_op jit(solution)/shard_map/while/body/eval_jaxpr/jit(_take)/gather | solution.py:78
  740.1 4.6 bitcast_select_fusion.2
  744.6 2.4 multiply_reduce_fusion.2
  747.0 3.5 fusion.31
  750.6 4.2 bitcast_dynamic-update-slice_fusion.2
  754.8 0.1 reshape.259
  754.9 0.1 broadcast_in_dim.101
  755.0 0.1 broadcast_in_dim.102
  755.1 8.5 %gather_fusion = bf16[128,64,256]{2,1,0:T(8,128)(2,1)} fusion(bf16[514,64,256]{2,1,0:T(8,128)(2,1)} %get-tuple-element.104, s32[1024]{0:T(1024)S(1)} %pad_clamp_fusion.4), kind=kCustom, calls=%fused_computation.clone.1 | custom fusion | bytes 8389120 | tf_op jit(solution)/shard_map/while/body/eval_jaxpr/jit(_take)/gather | solution.py:78
  763.7 4.6 bitcast_select_fusion.2
  768.2 2.4 multiply_reduce_fusion.2
  770.7 3.5 fusion.31
  774.2 4.2 bitcast_dynamic-update-slice_fusion.2
  778.5 0.1 reshape.259
  778.6 0.1 broadcast_in_dim.101
  778.6 0.1 broadcast_in_dim.102
  778.7 8.5 %gather_fusion = bf16[128,64,256]{2,1,0:T(8,128)(2,1)} fusion(bf16[514,64,256]{2,1,0:T(8,128)(2,1)} %get-tuple-element.104, s32[1024]{0:T(1024)S(1)} %pad_clamp_fusion.4), kind=kCustom, calls=%fused_computation.clone.1 | custom fusion | bytes 8389120 | tf_op jit(solution)/shard_map/while/body/eval_jaxpr/jit(_take)/gather | solution.py:78
  787.3 4.6 bitcast_select_fusion.2
  791.9 2.4 multiply_reduce_fusion.2
  794.3 3.5 fusion.31
  797.8 4.2 bitcast_dynamic-update-slice_fusion.2
  802.1 5.8 reshape.217
  (23 shorter events, 0.2 us)
Async XLA Ops:
  10.3 13.6 %all-to-all-start = ((s32[16,1,32]{2,1,0:T(1,128)}), s32[16,1,32]{2,1,0:T(1,128)S(1)}, u32[]{:S(2)}, u32[]{:S(2)}) async-start(s32[16,1,32]{2,1,0:T(1,128)} %bitcast.6), calls=%async_computation | async-start | bytes 16384 | tf_op jit(solution)/shard_map/all_to_all | solution.py:52
  29.8 372.6 %all-to-all-start.1 = ((bf16[16,32,64,256]{3,2,1,0:T(8,128)(2,1)}), bf16[16,32,64,256]{3,2,1,0:T(8,128)(2,1)}, u32[]{:S(2)}, u32[]{:S(2)}) async-start(bf16[16,32,64,256]{3,2,1,0:T(8,128)(2,1)} %stack.8), calls=%async_computation.1 | async-start | bytes 33554432 | tf_op jit(solution)/shard_map/all_to_all | solution.py:40
  436.0 6.6 copy-start
  436.0 281.1 %all-to-all-start.2 = ((bf16[16,32,64,256]{3,2,1,0:T(8,128)(2,1)}), bf16[16,32,64,256]{3,2,1,0:T(8,128)(2,1)}, u32[]{:S(2)}, u32[]{:S(2)}) async-start(bf16[16,32,64,256]{3,2,1,0:T(8,128)(2,1)} %broadcast_select_fusion), calls=%async_computation.2 | async-start | bytes 33554432 | tf_op jit(solution)/shard_map/all_to_all | solution.py:56
  442.5 274.6 %all-reduce.2.cloned.1.call-start = ((), (), s32[]{:S(2)}) async-start(), calls=%async_computation.3 | async-start | bytes 131072 | tf_op jit(solution)/shard_map/psum | solution.py:65
Sparse Core Ops, SparseCore 0:
  447.3 269.7 all-reduce.1
